TPU v7x, 256 devices: a whole 4x4x8 slice. The times are simulated.
256 devices in a mesh: date: 8 (over x, y_hi), path: 32 (over z, y_lo, core).
Axes of the slice: x: 4, y: 4 (y_hi: 2, y_lo: 2; y = y_hi * 2 + y_lo), z: 8, core: 2. Of those that a mesh axis runs over, the one named last changes fastest.
Arguments:
- factors: bfloat16 [64, 16, 131072], P('date', None, 'path'), may hold values from -10 to 10
- cashflows: bfloat16 [64, 64, 131072], P('date', None, 'path'), may hold values from -12 to 12
- frequency: bfloat16 [128, 16], replicated, may hold values from -1.5 to 1.5
- phases: float32 [128], replicated, may hold values from -3.140625 to 3.140625
- margin_lag: int32 [64], replicated, may hold values from 1 to 2
- thresholds: int32 [64], replicated, may hold values from 0 to 149
- transfer_min: int32 [64], replicated, may hold values from 0 to 59
Outputs:
- exposure: bfloat16 [64, 64, 131072], P('date', None, 'path')
- profile: float32 [64, 64], P('date')
All inputs are finite; a program needn't handle non-finite values.
Results may differ from a plain program's by a relative error of at most 0.0058.
Values may be sent and summed in bfloat16 or wider, within the bound.
No kernel may reach another device: no remote copies, remote signals or barrier semaphores. Data moves between devices by JAX's collectives and lax.ppermute only.
A program may use at most 128 MiB of HBM per device.

v0:
```python
import jax
import jax.numpy as jnp
from jax import lax
from jax.sharding import PartitionSpec as P

LAG_MAX = 2
ridge_weight = 0.05
root_two = 1.4142135623730951


def shifted_2(value, axis, by):
    length = lax.axis_size(axis)
    pairs = [(i, i + by) for i in range(length) if 0 <= i + by < length]
    return lax.ppermute(value, axis, pairs)


def packed_total(arrays, axis):
    ends = [0]
    for a in arrays:
        ends.append(ends[-1] + a.size)
    total = lax.psum(jnp.concatenate([a.ravel() for a in arrays]), axis)
    return tuple((total[b:e].reshape(a.shape) for a, b, e in zip(arrays, ends, ends[1:])))


def from_everyone(value, axis):
    length = lax.axis_size(axis)
    return lax.all_to_all(
        jnp.broadcast_to(value[None], (length, *value.shape)), axis, 0, 0, tiled=True
    )


def over_copies(value, axis):
    return from_everyone(value, axis).sum(axis=0)


def featurize(frequency, phases, factors):
    angles = jnp.einsum("kr,trp->tkp", frequency, factors, preferred_element_type=jnp.float32)
    angles = angles + phases[None, :, None]
    return (root_two * jnp.cos(angles)).astype(jnp.bfloat16)


def regress(gram_sum, right_sum, paths_all):
    system = (
        gram_sum / paths_all + ridge_weight * jnp.eye(gram_sum.shape[-1], dtype=jnp.float32)[None]
    )
    factor = lax.linalg.cholesky(system)
    solved = lax.linalg.triangular_solve(factor, right_sum / paths_all, left_side=True, lower=True)
    solved = lax.linalg.triangular_solve(
        factor, solved, left_side=True, lower=True, transpose_a=True
    )
    return solved.astype(jnp.bfloat16)


def fitted(coefficients, features):
    return jnp.einsum(
        "tkn,tkp->tnp", coefficients, features, preferred_element_type=jnp.float32
    ).astype(jnp.bfloat16)


def local(factors, cashflows, frequency, phases, margin_lag, thresholds, transfer_min):
    prior_factors = shifted_2(factors[-LAG_MAX:], "date", 1)
    features = featurize(frequency, phases, factors)
    gram_sum = jnp.einsum("tkp,tjp->tkj", features, features, preferred_element_type=jnp.float32)
    right_sum = jnp.einsum("tkp,tnp->tkn", features, cashflows, preferred_element_type=jnp.float32)
    gram_sum, right_sum = packed_total((gram_sum, right_sum), "path")
    paths_all = features.shape[2] * lax.axis_size("path")
    coefficients = regress(gram_sum, right_sum, paths_all)
    values = fitted(coefficients, features)
    prior_coefs = shifted_2(coefficients[-LAG_MAX:], "date", 1)
    prior_values = fitted(prior_coefs, featurize(frequency, phases, prior_factors))
    joined = jnp.concatenate([prior_values, values], axis=0)
    dates_here = values.shape[0]
    lagged = jnp.zeros(values.shape, jnp.float32)
    for lag_value in range(1, LAG_MAX + 1):
        shifted = joined[LAG_MAX - lag_value : LAG_MAX - lag_value + dates_here].astype(jnp.float32)
        lagged = jnp.where((margin_lag == lag_value)[None, :, None], shifted, lagged)
    offset = (thresholds + transfer_min).astype(jnp.float32) / 100.0
    collateral = jnp.maximum(lagged - offset[None, :, None], 0.0)
    exposure = jnp.maximum(values.astype(jnp.float32) - collateral, 0.0)
    profile = over_copies(jnp.sum(exposure, axis=2), "path") / paths_all
    return (exposure.astype(jnp.bfloat16), profile)


def solution(mesh):
    return jax.shard_map(
        local,
        mesh=mesh,
        in_specs=(P("date", None, "path"), P("date", None, "path"), P(), P(), P(), P(), P()),
        out_specs=(P("date", None, "path"), P("date", None)),
        check_vma=False,
    )
```

profile of v0, /device:TPU:1, one launch (start us, length us, event | category | flops | bytes accessed | tf_op | source)
XLA Modules:
  0.0 543.0 jit_solution(3618707060904881406)
XLA Ops:
  7.2 0.6 copy-done
  7.9 58.2 %multiply_convert_fusion = bf16[8,4096,128]{2,1,0:T(8,128)(2,1)S(1)} fusion(bf16[8,16,4096]{2,1,0:T(8,128)(2,1)} %param.7, f32[128]{0:T(128)} %param.10, bf16[128,16]{0,1:T(8,128)(2,1)S(1)} %copy-done), kind=kOutput, calls=%fused_computation | convolution fusion | flops 146800640 | bytes 9441792 | tf_op jit(solution)/shard_map/kr,trp->tkp/dot_general | solution.py:37
  66.1 2.5 fusion.13
  68.6 0.7 copy-done.1
  69.3 4.8 fusion.14
  74.3 0.9 pad_maximum_fusion.1
  75.3 1.0 slice.49
  76.2 6.1 %collective-permute-start.1 = (bf16[2,16,4096]{2,1,0:T(8,128)(2,1)S(1)}, bf16[2,16,4096]{2,1,0:T(8,128)(2,1)S(1)}, u32[]{:S(2)}, u32[]{:S(2)}) collective-permute-start(bf16[2,16,4096]{2,1,0:T(8,128)(2,1)S(1)} %slice.49), channel_id=1, source_target_pairs={{0,32},{32,64},{64,96},{96,128},{128,160},{160,192},{192,224},{1,3... | collective-permute-start | bytes 786440 | tf_op jit(solution)/shard_map/ppermute | solution.py:14
  82.6 222.5 %all-reduce.2.cloned.1.call-done = f32[196608]{0:T(1024)} async-done(((f32[196608]{0:T(1024)}), f32[196608]{0:T(1024)}) %all-reduce.2.cloned.1.call-update) | async-done | bytes 786448 | tf_op jit(solution)/shard_map/psum | solution.py:21
  305.1 1.1 slice_multiply_fusion
  306.2 0.2 copy.22
  306.7 93.8 %custom-call.8 = f32[8,128,128]{2,1,0:T(8,128)S(1)} custom-call(f32[8,128,128]{2,1,0:T(8,128)S(1)} %fusion.7), custom_call_target="Cholesky" | custom-call | tf_op jit(solution)/shard_map/cholesky | solution.py:46
  400.8 78.6 %custom-call.9 = f32[8,1,128,128]{2,3,1,0:T(8,128)S(1)} custom-call(f32[8,1,128,128]{3,2,1,0:T(8,128)S(1)} %select_bitcast_fusion), custom_call_target="InvertDiagBlocksLowerTriangular" | custom-call | tf_op jit(solution)/shard_map/triangular_solve | solution.py:48
  479.4 1.0 slice_multiply_fusion.1
  480.5 1.0 fusion.5
  481.6 1.1 convolution_convert_fusion.2
  482.7 4.5 collective-permute-start
  487.2 8.4 %convolution_convert_fusion = bf16[8,64,4096]{2,1,0:T(8,128)(2,1)} fusion(bf16[8,128,64]{1,2,0:T(8,128)(2,1)S(1)} %convolution_convert_fusion.2, bf16[8,4096,128]{2,1,0:T(8,128)(2,1)} %copy-done.1), kind=kOutput, calls=%fused_computation.2 | convolution fusion | flops 538968064 | bytes 12713984 | tf_op jit(solution)/shard_map/tkn,tkp->tnp/dot_general | solution.py:55
  495.6 14.6 %convolution_convert_fusion.1 = bf16[2,64,4096]{2,1,0:T(8,128)(2,1)S(1)} fusion(bf16[2,128,64]{1,2,0:T(8,128)(2,1)S(1)} %collective-permute-done, bf16[2,16,4096]{2,1,0:T(8,128)(2,1)S(1)} %collective-permute-done.1, f32[128]{0:T(128)S(1)} %copy-done.5, bf16[128,16]{0,1:T(8,128)(2,1)S(1)} %copy-done), kind=kOutput, calls=%fused_computation.9 | convolution fusion | flops 171442176 | bytes 1348096 | tf_op jit(solution)/shard_map/tkn,tkp->tnp/dot_general | solution.py:55
  510.2 7.9 %fusion.12 = (f32[8,64]{1,0:T(8,128)S(1)}, bf16[8,64,4096]{2,1,0:T(8,128)(2,1)}) fusion(f32[64]{0:T(128)S(1)} %convert_multiply_fusion, bf16[8,64,4096]{2,1,0:T(8,128)(2,1)} %convolution_convert_fusion, bf16[2,64,4096]{2,1,0:T(8,128)(2,1)S(1)} %convolution_convert_fusion.1, pred[64]{0:T(512)(128)(4,1)S(1)} %get-tuple-element.5, ...), kind=kLoop, calls=%fused_computation.35 | loop fusion | flops 27262464 | bytes 9439616 | tf_op jit(solution)/shard_map/reduce_sum | solution.py:80
  518.2 15.6 %all_to_all.5 = f32[32,1,512]{2,1,0:T(1,128)S(1)} all-to-all(f32[32,1,512]{2,1,0:T(1,128)S(1)} %reshape.60), channel_id=1, replica_groups=mesh['date'=8,'path'=32] {'path'}, dimensions={0} | all-to-all | bytes 131072 | tf_op jit(solution)/shard_map/all_to_all | solution.py:27
  533.9 0.5 broadcast.86
  534.4 0.8 reduce.4
  535.3 0.6 broadcast_multiply_fusion
  (33 shorter events, 1.4 us)
Async XLA Ops:
  7.2 0.7 copy-start
  7.2 297.9 %all-reduce.2.cloned.1.call-start = ((), (), s32[]{:S(2)}) async-start(), calls=%async_computation.1 | async-start | bytes 1572864 | tf_op jit(solution)/shard_map/psum | solution.py:21
  66.1 3.2 copy-start.1
  69.3 13.2 %copy-start.2 = (s32[64]{0:T(128)S(1)}, s32[64]{0:T(128)}, u32[]{:S(2)}) copy-start(s32[64]{0:T(128)} %param.11) | copy-start | bytes 772
  69.3 13.2 %copy-start.3 = (s32[64]{0:T(128)S(1)}, s32[64]{0:T(128)}, u32[]{:S(2)}) copy-start(s32[64]{0:T(128)} %param.12) | copy-start | bytes 772
  69.3 13.3 %copy-start.4 = (s32[64]{0:T(128)S(1)}, s32[64]{0:T(128)}, u32[]{:S(2)}) copy-start(s32[64]{0:T(128)} %param.13) | copy-start | bytes 772
  76.2 419.4 %collective-permute-start.1 = (bf16[2,16,4096]{2,1,0:T(8,128)(2,1)S(1)}, bf16[2,16,4096]{2,1,0:T(8,128)(2,1)S(1)}, u32[]{:S(2)}, u32[]{:S(2)}) collective-permute-start(bf16[2,16,4096]{2,1,0:T(8,128)(2,1)S(1)} %slice.49), channel_id=1, source_target_pairs={{0,32},{32,64},{64,96},{96,128},{128,160},{160,192},{192,224},{1,3... | collective-permute-start | bytes 786440 | tf_op jit(solution)/shard_map/ppermute | solution.py:14
  400.8 94.8 %copy-start.5 = (f32[128]{0:T(128)S(1)}, f32[128]{0:T(128)}, u32[]{:S(2)}) copy-start(f32[128]{0:T(128)} %param.10) | copy-start | bytes 1540
  482.7 12.9 %collective-permute-start = (bf16[2,128,64]{1,2,0:T(8,128)(2,1)S(1)}, bf16[2,128,64]{1,2,0:T(8,128)(2,1)S(1)}, u32[]{:S(2)}, u32[]{:S(2)}) collective-permute-start(bf16[2,128,64]{1,2,0:T(8,128)(2,1)S(1)} %slice.54), channel_id=1, source_target_pairs={{0,32},{32,64},{64,96},{96,128},{128,160},{160,192},{192,224},{1,3... | collective-permute-start | bytes 98312 | tf_op jit(solution)/shard_map/ppermute | solution.py:14
Sparse Core Ops, SparseCore 0:
  75.4 229.6 all-reduce.1
where the time goes:
time: 550 us; the launch traced here: 543 us
  waiting for transfers between devices  223 us (41%)
  other arithmetic  185 us (34%)
  matrix products  90.7 us (16%)
  blocking collectives  15.6 us (3%)
  between operations  14.5 us (3%)
  starting transfers between devices  10.7 us (2%)
    psum x1, waiting for transfers between devices, packed_total(): total = lax.psum(jnp.concatenate([a.ravel() for a in arrays]), axis)  222 us
    another operation x4, other arithmetic, regress(): factor = lax.linalg.cholesky(system)  94 us
    another operation x3, other arithmetic, regress(): lax.linalg.triangular_solve(factor, solved, left_side=True, lower=True, t...  78.7 us
    dot_general x1, matrix products, featurize(): jnp.einsum('kr,trp->tkp', frequency, factors, preferred_element_type=jnp....  58.2 us
    dot_general x2, matrix products, fitted(): jnp.einsum('tkn,tkp->tnp', coefficients, features, preferred_element_type...  23 us
    all_to_all x1, blocking collectives, from_everyone(): lax.all_to_all(jnp.broadcast_to(value[None], (length, *value.shape)), axi...  15.6 us
  transfers between devices with their start and end apart: 3, of which 1 were waited for; matrix products, arithmetic and copies ran while one was open for 34% of the time, Pallas kernels for 0%

commit v1 on v0

--- a/solution.py
+++ b/solution.py
@@ -6,6 +6,12 @@
 LAG_MAX = 2
 ridge_weight = 0.05
 root_two = 1.4142135623730951
+
+
+def gather_and_add(x, axis):
+    parts = lax.all_gather(x, axis, axis=0, tiled=False)
+    acc = parts.sum(axis=0)
+    return acc
 
 
 def shifted_2(value, axis, by):
@@ -18,7 +24,7 @@
     ends = [0]
     for a in arrays:
         ends.append(ends[-1] + a.size)
-    total = lax.psum(jnp.concatenate([a.ravel() for a in arrays]), axis)
+    total = gather_and_add(jnp.concatenate([a.ravel() for a in arrays]), axis)
     return tuple((total[b:e].reshape(a.shape) for a, b, e in zip(arrays, ends, ends[1:])))
 
 

time: 550 us -> 503 us (0.915)
  waiting for transfers between devices: 223 us -> 139 us
  local copies, waits for them, and re-layouts: 3.86 us -> 30.1 us
  other arithmetic: 185 us -> 195 us
    psum x1 -> x0, waiting for transfers between devices: 222 us -> none  [packed_total(): total = lax.psum(jnp.concatenate([a.ravel() for a in arrays]), axis)]
    all_gather x0 -> x1, waiting for transfers between devices: none -> 139 us  [gather_and_add(): parts = lax.all_gather(x, axis, axis=0, tiled=False)]
    all_gather x0 -> x1, local copies, waits for them, and re-layouts: none -> 26.2 us  [gather_and_add(): parts = lax.all_gather(x, axis, axis=0, tiled=False)]
    reduce_sum x0 -> x1, other arithmetic: none -> 12.3 us  [gather_and_add(): acc = parts.sum(axis=0)]
  transfers between devices with their start and end apart: 3 -> 3, of which waited for: 1 -> 1; matrix products, arithmetic and copies ran while one was open for 34% -> 45% of each run, Pallas kernels for 0% -> 0%
where the time goes in v1:
time: 503 us; the launch traced here: 496 us
  other arithmetic  195 us (39%)
  waiting for transfers between devices  139 us (28%)
  matrix products  90.6 us (18%)
  local copies, waits for them, and re-layouts  30.1 us (6%)
  blocking collectives  14.9 us (3%)
  between operations  14.5 us (3%)
  starting transfers between devices  11 us (2%)
    all_gather x1, waiting for transfers between devices, gather_and_add(): parts = lax.all_gather(x, axis, axis=0, tiled=False)  139 us
    another operation x4, other arithmetic, regress(): factor = lax.linalg.cholesky(system)  94 us
    another operation x3, other arithmetic, regress(): lax.linalg.triangular_solve(factor, solved, left_side=True, lower=True, t...  78.7 us
    dot_general x1, matrix products, featurize(): jnp.einsum('kr,trp->tkp', frequency, factors, preferred_element_type=jnp....  58.2 us
    all_gather x1, local copies, waits for them, and re-layouts, gather_and_add(): parts = lax.all_gather(x, axis, axis=0, tiled=False)  26.2 us
    dot_general x2, matrix products, fitted(): jnp.einsum('tkn,tkp->tnp', coefficients, features, preferred_element_type...  23 us
    all_to_all x1, blocking collectives, from_everyone(): lax.all_to_all(jnp.broadcast_to(value[None], (length, *value.shape)), axi...  14.9 us
    reduce_sum x1, other arithmetic, gather_and_add(): acc = parts.sum(axis=0)  12.3 us
  transfers between devices with their start and end apart: 3, of which 1 were waited for; matrix products, arithmetic and copies ran while one was open for 45% of the time, Pallas kernels for 0%

profile of v1, /device:TPU:1, one launch (start us, length us, event | category | flops | bytes accessed | tf_op | source)
XLA Modules:
  0.0 495.5 jit_solution(1922192161066481538)
XLA Ops:
  7.2 0.6 copy-done
  7.9 58.2 %multiply_convert_fusion = bf16[8,4096,128]{2,1,0:T(8,128)(2,1)S(1)} fusion(bf16[8,16,4096]{2,1,0:T(8,128)(2,1)} %param.7, f32[128]{0:T(128)} %param.10, bf16[128,16]{0,1:T(8,128)(2,1)S(1)} %copy-done), kind=kOutput, calls=%fused_computation | convolution fusion | flops 146800640 | bytes 9441792 | tf_op jit(solution)/shard_map/kr,trp->tkp/dot_general | solution.py:43
  66.1 2.5 fusion.13
  68.6 0.7 copy-done.1
  69.3 4.8 fusion.14
  74.3 0.9 pad_maximum_fusion.1
  75.3 1.0 slice.49
  76.2 6.1 %collective-permute-start.1 = (bf16[2,16,4096]{2,1,0:T(8,128)(2,1)S(1)}, bf16[2,16,4096]{2,1,0:T(8,128)(2,1)S(1)}, u32[]{:S(2)}, u32[]{:S(2)}) collective-permute-start(bf16[2,16,4096]{2,1,0:T(8,128)(2,1)S(1)} %slice.49), channel_id=1, source_target_pairs={{0,32},{32,64},{64,96},{96,128},{128,160},{160,192},{192,224},{1,3... | collective-permute-start | bytes 786440 | tf_op jit(solution)/shard_map/ppermute | solution.py:20
  82.6 139.0 %all-gather.3.cloned.1.call-done = f32[6291456]{0:T(1024)} async-done(((f32[196608]{0:T(1024)}), f32[6291456]{0:T(1024)}) %all-gather.3.cloned.1.call-update) | async-done | bytes 25165840 | tf_op jit(solution)/shard_map/all_gather | solution.py:12
  221.6 26.2 %reshape.59 = f32[32,196608]{1,0:T(8,128)} reshape(f32[6291456]{0:T(1024)} %all-gather.3.cloned.1.call-done) | data formatting | bytes 50331648 | tf_op jit(solution)/shard_map/all_gather | solution.py:12
  247.8 12.3 %reduce_sum.27 = f32[196608]{0:T(1024)S(1)} reduce(f32[32,196608]{1,0:T(8,128)} %reshape.59, f32[]{:T(128)} %constant.48.clone.1), dimensions={0}, to_apply=%region_0.0 | reduce | flops 6094848 | bytes 25952260 | tf_op jit(solution)/shard_map/reduce_sum | solution.py:13
  260.3 0.2 copy.30
  260.8 93.8 %custom-call.8 = f32[8,128,128]{2,1,0:T(8,128)S(1)} custom-call(f32[8,128,128]{2,1,0:T(8,128)S(1)} %fusion.7), custom_call_target="Cholesky" | custom-call | tf_op jit(solution)/shard_map/cholesky | solution.py:52
  354.9 78.6 %custom-call.9 = f32[8,1,128,128]{2,3,1,0:T(8,128)S(1)} custom-call(f32[8,1,128,128]{3,2,1,0:T(8,128)S(1)} %select_bitcast_fusion), custom_call_target="InvertDiagBlocksLowerTriangular" | custom-call | tf_op jit(solution)/shard_map/triangular_solve | solution.py:54
  433.6 1.0 fusion.5
  434.7 1.1 convolution_convert_fusion.2
  435.8 4.8 collective-permute-start
  440.6 8.3 %convolution_convert_fusion = bf16[8,64,4096]{2,1,0:T(8,128)(2,1)} fusion(bf16[8,128,64]{1,2,0:T(8,128)(2,1)S(1)} %convolution_convert_fusion.2, bf16[8,4096,128]{2,1,0:T(8,128)(2,1)} %copy-done.1), kind=kOutput, calls=%fused_computation.2 | convolution fusion | flops 538968064 | bytes 12713984 | tf_op jit(solution)/shard_map/tkn,tkp->tnp/dot_general | solution.py:61
  448.9 14.6 %convolution_convert_fusion.1 = bf16[2,64,4096]{2,1,0:T(8,128)(2,1)S(1)} fusion(bf16[2,128,64]{1,2,0:T(8,128)(2,1)S(1)} %collective-permute-done, bf16[2,16,4096]{2,1,0:T(8,128)(2,1)S(1)} %collective-permute-done.1, f32[128]{0:T(128)S(1)} %copy-done.5, bf16[128,16]{0,1:T(8,128)(2,1)S(1)} %copy-done), kind=kOutput, calls=%fused_computation.9 | convolution fusion | flops 171442176 | bytes 1348096 | tf_op jit(solution)/shard_map/tkn,tkp->tnp/dot_general | solution.py:61
  463.6 7.8 %fusion.12 = (f32[8,64]{1,0:T(8,128)S(1)}, bf16[8,64,4096]{2,1,0:T(8,128)(2,1)}) fusion(f32[64]{0:T(128)S(1)} %convert_multiply_fusion, bf16[8,64,4096]{2,1,0:T(8,128)(2,1)} %convolution_convert_fusion, bf16[2,64,4096]{2,1,0:T(8,128)(2,1)S(1)} %convolution_convert_fusion.1, pred[64]{0:T(512)(128)(4,1)S(1)} %get-tuple-element.5, ...), kind=kLoop, calls=%fused_computation.35 | loop fusion | flops 27262464 | bytes 9439616 | tf_op jit(solution)/shard_map/reduce_sum | solution.py:86
  471.5 14.9 %all_to_all.5 = f32[32,1,512]{2,1,0:T(1,128)S(1)} all-to-all(f32[32,1,512]{2,1,0:T(1,128)S(1)} %reshape.61), channel_id=1, replica_groups=mesh['date'=8,'path'=32] {'path'}, dimensions={0} | all-to-all | bytes 131072 | tf_op jit(solution)/shard_map/all_to_all | solution.py:33
  486.4 0.5 broadcast.86
  486.9 0.8 reduce.4
  487.9 0.6 broadcast_multiply_fusion
  (35 shorter events, 1.4 us)
Async XLA Ops:
  7.2 0.7 copy-start
  7.2 214.4 %all-gather.3.cloned.1.call-start = ((), (), s32[]{:S(2)}) async-start(), calls=%async_computation.1 | async-start | bytes 25952256 | tf_op jit(solution)/shard_map/all_gather | solution.py:12
  66.1 3.2 copy-start.1
  69.3 13.2 %copy-start.2 = (s32[64]{0:T(128)S(1)}, s32[64]{0:T(128)}, u32[]{:S(2)}) copy-start(s32[64]{0:T(128)} %param.11) | copy-start | bytes 772
  69.3 13.2 %copy-start.3 = (s32[64]{0:T(128)S(1)}, s32[64]{0:T(128)}, u32[]{:S(2)}) copy-start(s32[64]{0:T(128)} %param.12) | copy-start | bytes 772
  69.3 13.3 %copy-start.4 = (s32[64]{0:T(128)S(1)}, s32[64]{0:T(128)}, u32[]{:S(2)}) copy-start(s32[64]{0:T(128)} %param.13) | copy-start | bytes 772
  76.2 372.7 %collective-permute-start.1 = (bf16[2,16,4096]{2,1,0:T(8,128)(2,1)S(1)}, bf16[2,16,4096]{2,1,0:T(8,128)(2,1)S(1)}, u32[]{:S(2)}, u32[]{:S(2)}) collective-permute-start(bf16[2,16,4096]{2,1,0:T(8,128)(2,1)S(1)} %slice.49), channel_id=1, source_target_pairs={{0,32},{32,64},{64,96},{96,128},{128,160},{160,192},{192,224},{1,3... | collective-permute-start | bytes 786440 | tf_op jit(solution)/shard_map/ppermute | solution.py:20
  354.7 94.2 %copy-start.5 = (f32[128]{0:T(128)S(1)}, f32[128]{0:T(128)}, u32[]{:S(2)}) copy-start(f32[128]{0:T(128)} %param.10) | copy-start | bytes 1540
  435.8 13.1 %collective-permute-start = (bf16[2,128,64]{1,2,0:T(8,128)(2,1)S(1)}, bf16[2,128,64]{1,2,0:T(8,128)(2,1)S(1)}, u32[]{:S(2)}, u32[]{:S(2)}) collective-permute-start(bf16[2,128,64]{1,2,0:T(8,128)(2,1)S(1)} %slice.54), channel_id=1, source_target_pairs={{0,32},{32,64},{64,96},{96,128},{128,160},{160,192},{192,224},{1,3... | collective-permute-start | bytes 98312 | tf_op jit(solution)/shard_map/ppermute | solution.py:20
Sparse Core Ops, SparseCore 0:
  75.4 146.1 all-gather.2
